TPU v7x, 512 devices: a whole 4x4x16 slice. The times are simulated.
512 devices in a mesh: beam: 16 (over y, x), ma: 32 (over z, core).
Axes of the slice: x: 4, y: 4, z: 16, core: 2. Of those that a mesh axis runs over, the one named last changes fastest.
Arguments:
- sky_harmonics: float32 [64, 2, 2048], P('ma'), may hold values from -6 to 6
- beam_harmonics: float32 [128, 2, 2048], P('beam'), may hold values from -6 to 6
- wigner: bfloat16 [128, 64, 64, 2048], P('beam', 'ma'), may hold values from -0.125 to 0.125
- order_map: int32 [64], replicated, may hold values from 0 to 2047, as said below
- block_owner: int32 [4096, 1], P('ma'), may hold values from 0 to 31; in each aligned block of 128 rows (0 to 127, 128 to 255, ...) at most 8 rows name the same one
- block_local: int32 [4096], P('ma'), may hold values from 0 to 63
- cell_offset: int32 [524288], P('ma'), may hold values from 0 to 126
- cell_fraction: float32 [524288], P('ma'), may hold values from 0 to 1
- beam_angle: float32 [524288], P('ma'), may hold values from -3.140625 to 3.140625
- sample_count: int32 [32], P('ma'), may hold values from 1 to 16384, 393216 in all
- noise_weight: float32 [128, 128], replicated, may hold values from -0.2 to 2, as said below
Outputs:
- sky_gradient: float32 [64, 2, 2048], P('ma', None, 'beam')
Inputs may be any that keep to these rules, and one draw needn't show every extreme that they name: `order_map`: 64 distinct azimuthal orders. `block_owner`: among the 128 sample blocks of one device, at most 8 name the same owner, and in some device some owner is named exactly 8 times. `noise_weight`: diagonal entries lie in 1 to 2, the others within 0.2 in magnitude.
All inputs are finite; a program needn't handle non-finite values. No bound on the sum of `sample_count` on one device may be relied on, other than what follows from the above.
Results may differ from a plain program's by a relative error of at most 0.017.
Values may be sent and summed in bfloat16 or wider, within the bound.
A program may use at most 128 MiB of HBM per device.

v0:
```python
import math
import jax
import jax.numpy as jnp
from jax import lax
from jax.sharding import PartitionSpec as P

PHI = 4096
CELLS = 128


def copy_for_each(array, axis):
    devices = lax.axis_size(axis)
    return lax.all_to_all(
        jnp.broadcast_to(array[None], (devices, *array.shape)), axis, 0, 0, tiled=True
    )


def of_everyone(array, axis):
    return copy_for_each(array, axis).astype(jnp.float32).sum(axis=0)


def split_up(array, dim, devices):
    shape = array.shape
    blocks = array.reshape(*shape[:dim], devices, shape[dim] // devices, *shape[dim + 1 :])
    return jnp.moveaxis(blocks, dim, 0)


def summed_on_arrival(array, axis, dim):
    blocks = split_up(array, dim, lax.axis_size(axis))
    arrived = lax.all_to_all(blocks, axis, split_axis=0, concat_axis=0, tiled=True)
    return arrived.astype(jnp.float32).sum(axis=0)


def cycle_phases(order_map, cycle_cells):
    stepped = jnp.arange(cycle_cells, dtype=jnp.int32)
    phase_turns = order_map[:, None] * stepped[None, :] % cycle_cells
    angles = phase_turns.astype(jnp.float32) * (2.0 * math.pi / cycle_cells)
    scaling = 1.0 / math.sqrt(order_map.shape[0])
    return jnp.stack([jnp.cos(angles), -jnp.sin(angles)], axis=1) * scaling


def rotation(beam_order, beam_angle, total_orders):
    spin_order = ((beam_order + 1) // 2).astype(jnp.float32)
    angles = spin_order * beam_angle
    return jnp.where(beam_order % 2 == 0, jnp.cos(angles), jnp.sin(angles)) / math.sqrt(
        total_orders
    )


def harmonic_product(sky_harmonics, beam_harmonics):
    sky_real = sky_harmonics[None, :, 0]
    sky_imag = sky_harmonics[None, :, 1]
    beam_real = beam_harmonics[:, None, 0]
    beam_imag = beam_harmonics[:, None, 1]
    first = sky_real * beam_real - sky_imag * beam_imag
    second = sky_real * beam_imag + sky_imag * beam_real
    return jnp.stack([first, second], axis=2).astype(jnp.bfloat16)


def gradient_terms(grad_harmonics, beam_harmonics):
    grad_real = grad_harmonics[:, :, 0]
    grad_imag = grad_harmonics[:, :, 1]
    beam_real = beam_harmonics[:, None, 0]
    beam_imag = beam_harmonics[:, None, 1]
    first = jnp.sum(grad_real * beam_real + grad_imag * beam_imag, axis=0)
    second = jnp.sum(grad_imag * beam_real - grad_real * beam_imag, axis=0)
    return jnp.stack([first, second], axis=1)


def interpolate(flat_values, flat_low, fractions):
    return (1.0 - fractions) * flat_values[:, flat_low] + fractions * flat_values[:, flat_low + 1]


def spread(weighted, flat_low, fractions, span_cells):
    blank_grid = jnp.zeros((weighted.shape[0], span_cells), jnp.float32)
    blank_grid = blank_grid.at[:, flat_low].add((1.0 - fractions) * weighted)
    return blank_grid.at[:, flat_low + 1].add(fractions * weighted)


def local(
    sky_harmonics,
    beam_harmonics,
    wigner,
    order_map,
    block_owner,
    block_local,
    cell_offset,
    cell_fraction,
    beam_angle,
    sample_count,
    noise_weight,
):
    highest = lax.Precision.HIGHEST
    ma_count = lax.axis_size("ma")
    beam_count = lax.axis_size("beam")
    local_orders = beam_harmonics.shape[0]
    total_orders = local_orders * beam_count
    cycle_cells = PHI
    block_cells = CELLS
    sample_blocks = block_owner.shape[0]
    capacity = 2 * sample_blocks // ma_count
    cycle_count = wigner.shape[2]
    cycles_local = cycle_count // ma_count
    blocks_local = cycles_local * cycle_cells // block_cells
    product = harmonic_product(sky_harmonics, beam_harmonics)
    cycle_modes = jnp.einsum("kmcl,kmrl->kmcr", product, wigner, preferred_element_type=jnp.float32)
    slab_modes = lax.all_to_all(cycle_modes, "ma", split_axis=3, concat_axis=1, tiled=True)
    phase_table = cycle_phases(order_map, cycle_cells)
    cycle_cube = jnp.einsum("kmcr,mcp->krp", slab_modes, phase_table, precision=highest)
    owners = block_owner[:, 0]
    owner_hot = (owners[:, None] == jnp.arange(ma_count, dtype=jnp.int32)[None, :]).astype(
        jnp.int32
    )
    slot_rank = jnp.sum((jnp.cumsum(owner_hot, axis=0) - owner_hot) * owner_hot, axis=1)
    slot_index = owners * capacity + slot_rank
    requests = jnp.full((ma_count * capacity,), -1, jnp.int32).at[slot_index].set(block_local)
    requests = requests.reshape(ma_count, capacity)
    offsets = cell_offset.reshape(sample_blocks, block_cells)
    fractions = cell_fraction.reshape(sample_blocks, block_cells)
    angles = beam_angle.reshape(sample_blocks, block_cells)
    beam_order = lax.axis_index("beam") * local_orders + jnp.arange(local_orders, dtype=jnp.int32)
    stamps = jnp.arange(sample_blocks * block_cells, dtype=jnp.int32).reshape(
        sample_blocks, block_cells
    )
    valid_mask = (stamps < sample_count[0]).astype(jnp.float32)
    wanted = lax.all_to_all(requests, "ma", split_axis=0, concat_axis=0, tiled=True)
    wanted_flat = wanted.reshape(-1)
    outgoing = jnp.take(
        cycle_cube.reshape(local_orders, blocks_local, block_cells),
        jnp.clip(wanted_flat, 0, blocks_local - 1),
        axis=1,
    )
    outgoing = outgoing * (wanted_flat >= 0).astype(jnp.float32)[None, :, None]
    incoming = lax.all_to_all(
        outgoing.reshape(local_orders, ma_count, capacity, block_cells).astype(jnp.bfloat16),
        "ma",
        split_axis=1,
        concat_axis=1,
        tiled=True,
    ).astype(jnp.float32)
    blocks = jnp.take(
        incoming.reshape(local_orders, ma_count * capacity, block_cells), slot_index, axis=1
    )
    own_low = jnp.arange(sample_blocks, dtype=jnp.int32)[:, None] * block_cells + offsets
    own_turn = rotation(beam_order[:, None, None], angles[None], total_orders)
    values = interpolate(
        blocks.reshape(local_orders, sample_blocks * block_cells), own_low, fractions
    )
    partial_value = jnp.sum(own_turn * values, axis=0)
    signal = (
        of_everyone(partial_value.astype(jnp.bfloat16), "beam").astype(jnp.float32) * valid_mask
    )
    filtered = jnp.einsum("bu,tu->bt", signal, noise_weight, precision=highest) * valid_mask
    weighted = own_turn * filtered[None]
    own_spread = spread(weighted, own_low, fractions, sample_blocks * block_cells)
    own_spread = own_spread.reshape(local_orders, sample_blocks, block_cells)
    back_slots = (
        jnp.zeros((local_orders, ma_count * capacity, block_cells), jnp.float32)
        .at[:, slot_index]
        .set(own_spread)
    )
    arrived = lax.all_to_all(
        back_slots.reshape(local_orders, ma_count, capacity, block_cells).astype(jnp.bfloat16),
        "ma",
        split_axis=1,
        concat_axis=1,
        tiled=True,
    ).astype(jnp.float32)
    chooser = (wanted_flat[None, :] == jnp.arange(blocks_local, dtype=jnp.int32)[:, None]).astype(
        jnp.float32
    )
    cube_grad = jnp.einsum(
        "gs,ksc->kgc",
        chooser,
        arrived.reshape(local_orders, ma_count * capacity, block_cells),
        precision=highest,
    )
    cube_grad = cube_grad.reshape(local_orders, cycles_local, cycle_cells)
    grad_modes = jnp.einsum("krp,mcp->kmcr", cube_grad, phase_table, precision=highest).astype(
        jnp.bfloat16
    )
    grad_cycles = lax.all_to_all(grad_modes, "ma", split_axis=1, concat_axis=3, tiled=True)
    grad_harmonics = jnp.einsum(
        "kmcr,kmrl->kmcl", grad_cycles, wigner, preferred_element_type=jnp.float32
    )
    gradient = gradient_terms(grad_harmonics, beam_harmonics)
    result = summed_on_arrival(gradient.astype(jnp.bfloat16), "beam", 2)
    return result


def solution(mesh):
    return jax.shard_map(
        local,
        mesh=mesh,
        in_specs=(
            P("ma", None, None),
            P("beam", None, None),
            P("beam", "ma", None, None),
            P(),
            P("ma", None),
            P("ma"),
            P("ma"),
            P("ma"),
            P("ma"),
            P("ma"),
            P(),
        ),
        out_specs=P("ma", None, "beam"),
        check_vma=False,
    )
```

profile of v0, /device:TPU:2, one launch (start us, length us, event | category | flops | bytes accessed | tf_op | source)
XLA Modules:
  0.0 597.7 jit_solution(5402851796727341372)
XLA Ops:
  0.0 0.8 fusion.45
  1.0 0.8 select_reduce_fusion
  1.8 1.2 and_bitcast_fusion
  3.0 1.1 scatter_custom_fusion
  4.1 0.7 all_to_all.44
  4.8 15.5 %all-to-all-start = ((s32[32,1,8]{2,1,0:T(1,128)}), s32[32,1,8]{2,1,0:T(1,128)S(1)}, u32[]{:S(2)}, u32[]{:S(2)}) async-start(s32[32,1,8]{2,1,0:T(1,128)} %bitcast.12), calls=%async_computation | async-start | bytes 32768 | tf_op jit(solution)/shard_map/all_to_all | solution.py:126
  20.3 1.1 fusion.69
  21.4 0.9 fusion.70
  22.2 4.8 fusion.31
  27.5 3.4 fusion.34
  30.8 0.8 copy.89
  31.6 1.1 all-to-all-done
  32.7 11.0 %all-to-all-start.1 = ((f32[8,2,2,64]{0,2,1,3:T(2,128)}), f32[8,2,2,64]{0,2,1,3:T(2,128)S(1)}, u32[]{:S(2)}, u32[]{:S(2)}) async-start(f32[8,2,2,64]{0,2,1,3:T(2,128)} %copy.89), calls=%async_computation.1 | async-start | bytes 262144 | tf_op jit(solution)/shard_map/all_to_all | solution.py:107
  44.4 1.3 fusion.65
  45.7 0.6 compare_and_fusion
  46.4 0.6 pad_clamp_fusion.1
  47.0 14.0 %all-to-all-done.1 = f32[8,2,2,64]{0,2,1,3:T(2,128)S(1)} async-done(((f32[8,2,2,64]{0,2,1,3:T(2,128)}), f32[8,2,2,64]{0,2,1,3:T(2,128)S(1)}, u32[]{:S(2)}, u32[]{:S(2)}) %all-to-all-start.1) | async-done | bytes 8224 | tf_op jit(solution)/shard_map/all_to_all | solution.py:107
  61.1 1.2 fusion.12
  62.3 1.2 gather_fusion
  63.4 2.1 multiply_convert_fusion
  65.5 4.8 all-to-all-start.2
  70.4 0.6 pad_clamp_fusion
  71.0 0.7 broadcast_bitcast_fusion
  71.7 1.6 broadcast_clamp_fusion
  73.3 30.8 %all-to-all-done.2 = bf16[8,32,8,128]{3,0,2,1:T(8,128)(2,1)} async-done(((bf16[8,32,8,128]{3,0,2,1:T(8,128)(2,1)}), bf16[8,32,8,128]{3,0,2,1:T(8,128)(2,1)}, u32[]{:S(2)}, u32[]{:S(2)}) %all-to-all-start.2) | async-done | bytes 524320 | tf_op jit(solution)/shard_map/all_to_all | solution.py:134
  104.1 1.1 bitcast_convert_fusion
  105.2 1.5 gather_fusion.1
  106.8 5.7 copy.95
  112.4 13.1 %broadcast_select_fusion = f32[8,16384]{0,1:T(8,128)} fusion(f32[8,16384]{0,1:T(8,128)} %copy.95, pred[16384]{0:T(1024)(128)(4,1)S(1)} %broadcast_bitcast_fusion), kind=kLoop, calls=%fused_computation.17 | loop fusion | flops 131072 | bytes 1064960 | tf_op jit(solution)/shard_map/jit(_take)/select_n | solution.py:141
  125.5 57.8 %gather_fusion.2 = f32[16384,8]{1,0:T(8,128)} fusion(f32[8,16384]{0,1:T(8,128)} %broadcast_select_fusion, s32[16384]{0:T(1024)S(1)} %copy-done.7), kind=kCustom, calls=%fused_computation.2 | custom fusion | bytes 1114112 | tf_op jit(solution)/shard_map/gather | solution.py:71
  183.3 57.8 %gather_fusion.3 = f32[16384,8]{1,0:T(8,128)} fusion(f32[8,16384]{0,1:T(8,128)} %broadcast_select_fusion, s32[16384]{0:T(1024)S(1)} %get-tuple-element.11), kind=kCustom, calls=%fused_computation.3 | custom fusion | bytes 1114112 | tf_op jit(solution)/shard_map/gather | solution.py:71
  241.1 39.0 %fusion.6 = bf16[128,128]{1,0:T(8,128)(2,1)S(1)} fusion(f32[128,128,8]{2,1,0:T(8,128)} %bitcast.131, f32[128,128,8]{2,1,0:T(8,128)} %bitcast.130, f32[128,128]{1,0:T(8,128)S(1)} %bitcast.138, f32[128,128]{1,0:T(8,128)S(1)} %broadcast_subtract_fusion, f32[128,128]{1,0:T(8,128)S(1)} %bitcast.142, f32[8]{0:T(128)S(1)} %fusion.56, pred[8]{0:T(512)(128)(4,1)S(1)} %fusion.52), kind=kLoop, calls=%fused_computation.16 | loop fusion | flops 1032192 | bytes 1277992 | tf_op jit(solution)/shard_map/reduce_sum | solution.py:149
  280.1 0.9 broadcast_in_dim.73
  281.0 7.5 %all-to-all-start.3 = ((bf16[16,128,128]{2,1,0:T(8,128)(2,1)}), bf16[16,128,128]{2,1,0:T(8,128)(2,1)S(1)}, u32[]{:S(2)}, u32[]{:S(2)}) async-start(bf16[16,128,128]{2,1,0:T(8,128)(2,1)} %broadcast_in_dim.73), calls=%async_computation.3 | async-start | bytes 1048576 | tf_op jit(solution)/shard_map/all_to_all | solution.py:13
  289.1 9.4 %all-to-all-done.3 = bf16[16,128,128]{2,1,0:T(8,128)(2,1)S(1)} async-done(((bf16[16,128,128]{2,1,0:T(8,128)(2,1)}), bf16[16,128,128]{2,1,0:T(8,128)(2,1)S(1)}, u32[]{:S(2)}, u32[]{:S(2)}) %all-to-all-start.3) | async-done | bytes 524320 | tf_op jit(solution)/shard_map/all_to_all | solution.py:13
  298.9 33.4 %fusion.3 = (f32[8,128,128]{0,2,1:T(8,128)}, f32[8,128,128]{0,2,1:T(8,128)}) fusion(f32[128,128]{1,0:T(8,128)S(1)} %fusion.14, f32[128,128]{1,0:T(8,128)S(1)} %bitcast.139, f32[128,128]{1,0:T(8,128)S(1)} %bitcast.143, f32[8]{0:T(128)S(1)} %fusion.56, pred[8]{0:T(512)(128)(4,1)S(1)} %fusion.52, f32[128,128]{1,0:T(8,128)S(1)} %broadcast_subtract_fusion), kind=kLoop, calls=%fused_computation.13 | loop fusion | flops 655360 | bytes 1310760 | tf_op jit(solution)/shard_map/mul | solution.py:77
  332.3 91.3 %scatter_custom_fusion.1 = f32[8,16384]{0,1:T(8,128)} fusion(s32[16384]{0:T(1024)} %get-tuple-element.24, f32[16384,8]{1,0:T(8,128)} %bitcast.132, f32[]{:T(128)} %constant.97.clone.1), kind=kCustom, calls=%fused_computation.18 | custom fusion | flops 131072 | bytes 524800 | tf_op jit(solution)/shard_map/scatter-add | solution.py:76
  423.6 85.3 %scatter_fusion = f32[8,16384]{0,1:T(8,128)} fusion(f32[8,16384]{0,1:T(8,128)} %scatter_custom_fusion.1, s32[16384]{0:T(1024)S(1)} %get-tuple-element.12, f32[16384,8]{1,0:T(8,128)} %bitcast.129), kind=kCustom, calls=%fused_computation.6 | custom fusion | flops 131072 | bytes 1638400 | tf_op jit(solution)/shard_map/scatter-add | solution.py:77
  508.9 5.9 copy.96
  514.9 8.7 %scatter_fusion.1 = f32[8,256,128]{2,0,1:T(8,128)S(1)} fusion(f32[8,256,128]{2,0,1:T(8,128)S(1)} %broadcast_in_dim.40, s32[128]{0:T(128)S(1)} %bitcast.154, f32[128,8,128]{2,1,0:T(8,128)} %bitcast.135), kind=kCustom, calls=%fused_computation.7 | custom fusion | bytes 1573376 | tf_op jit(solution)/shard_map/scatter | solution.py:160
  523.7 0.9 copy.97
  524.5 4.1 all-to-all-start.4
  528.8 33.9 %all-to-all-done.4 = bf16[8,32,8,128]{3,2,0,1:T(8,128)(2,1)S(1)} async-done(((bf16[8,32,8,128]{3,2,0,1:T(8,128)(2,1)}), bf16[8,32,8,128]{3,2,0,1:T(8,128)(2,1)S(1)}, u32[]{:S(2)}, u32[]{:S(2)}) %all-to-all-start.4) | async-done | bytes 524320 | tf_op jit(solution)/shard_map/all_to_all | solution.py:162
  563.0 2.5 fusion.18
  565.7 17.3 %all_to_all.65 = bf16[8,64,2,2]{0,3,2,1:T(2,128)(2,1)S(1)} all-to-all(bf16[8,64,2,2]{0,3,2,1:T(2,128)(2,1)S(1)} %copy.100), channel_id=1, replica_groups=mesh['beam'=16,'ma'=32] {'ma'}, dimensions={1} | all-to-all | bytes 8192 | tf_op jit(solution)/shard_map/all_to_all | solution.py:182
  583.2 2.8 fusion.71
  586.5 10.5 %all_to_all.66 = bf16[16,2,2,128]{3,1,2,0:T(2,128)(2,1)S(1)} all-to-all(bf16[16,2,2,128]{3,1,2,0:T(2,128)(2,1)S(1)} %maximum_bitcast_fusion), channel_id=1, replica_groups=mesh['beam'=16,'ma'=32] {'beam'}, dimensions={0} | all-to-all | bytes 32768 | tf_op jit(solution)/shard_map/all_to_all | solution.py:30
  597.1 0.6 copy.105
  (51 shorter events, 3.1 us)
Async XLA Ops:
  0.0 298.6 %copy-start = (f32[128,128]{1,0:T(8,128)S(1)}, f32[128,128]{1,0:T(8,128)}, u32[]{:S(2)}) copy-start(f32[128,128]{1,0:T(8,128)} %param.21) | copy-start | bytes 196612
  0.0 71.0 %copy-start.1 = (f32[16384]{0:T(1024)S(1)}, f32[16384]{0:T(1024)}, u32[]{:S(2)}) copy-start(f32[16384]{0:T(1024)} %param.18) | copy-start | bytes 196612
  3.0 18.4 %copy-start.9 = (s32[128,1]{0,1:T(1,128)}, s32[128,1]{0,1:T(1,128)S(1)}, u32[]{:S(2)}) copy-start(s32[128,1]{0,1:T(1,128)S(1)} %get-tuple-element.14) | copy-start | bytes 1540
  4.8 28.0 %all-to-all-start = ((s32[32,1,8]{2,1,0:T(1,128)}), s32[32,1,8]{2,1,0:T(1,128)S(1)}, u32[]{:S(2)}, u32[]{:S(2)}) async-start(s32[32,1,8]{2,1,0:T(1,128)} %bitcast.12), calls=%async_computation | async-start | bytes 32768 | tf_op jit(solution)/shard_map/all_to_all | solution.py:126
  27.1 34.0 %copy-start.2 = (f32[8,2048]{1,0:T(8,128)}, f32[8,2048]{1,0:T(8,128)S(1)}, u32[]{:S(2)}) copy-start(f32[8,2048]{1,0:T(8,128)S(1)} %get-tuple-element.30) | copy-start | bytes 196612
  27.1 34.0 %copy-start.4 = (f32[8,2048]{1,0:T(8,128)}, f32[8,2048]{1,0:T(8,128)S(1)}, u32[]{:S(2)}) copy-start(f32[8,2048]{1,0:T(8,128)S(1)} %get-tuple-element.31) | copy-start | bytes 196612
  32.7 28.2 %all-to-all-start.1 = ((f32[8,2,2,64]{0,2,1,3:T(2,128)}), f32[8,2,2,64]{0,2,1,3:T(2,128)S(1)}, u32[]{:S(2)}, u32[]{:S(2)}) async-start(f32[8,2,2,64]{0,2,1,3:T(2,128)} %copy.89), calls=%async_computation.1 | async-start | bytes 262144 | tf_op jit(solution)/shard_map/all_to_all | solution.py:107
  65.5 38.6 %all-to-all-start.2 = ((bf16[8,32,8,128]{3,0,2,1:T(8,128)(2,1)}), bf16[8,32,8,128]{3,0,2,1:T(8,128)(2,1)}, u32[]{:S(2)}, u32[]{:S(2)}) async-start(bf16[8,32,8,128]{3,0,2,1:T(8,128)(2,1)} %multiply_convert_fusion), calls=%async_computation.2 | async-start | bytes 1048576 | tf_op jit(solution)/shard_map/all_to_all | solution.py:134
  112.4 13.1 %copy-start.7 = (s32[16384]{0:T(1024)S(1)}, s32[16384]{0:T(1024)}, u32[]{:S(2)}) copy-start(s32[16384]{0:T(1024)} %get-tuple-element.23) | copy-start | bytes 196612
  125.5 115.6 %copy-start.6 = (f32[16384]{0:T(1024)S(1)}, f32[16384]{0:T(1024)}, u32[]{:S(2)}) copy-start(f32[16384]{0:T(1024)} %param.19) | copy-start | bytes 196612
  281.0 17.5 %all-to-all-start.3 = ((bf16[16,128,128]{2,1,0:T(8,128)(2,1)}), bf16[16,128,128]{2,1,0:T(8,128)(2,1)S(1)}, u32[]{:S(2)}, u32[]{:S(2)}) async-start(bf16[16,128,128]{2,1,0:T(8,128)(2,1)} %broadcast_in_dim.73), calls=%async_computation.3 | async-start | bytes 1048576 | tf_op jit(solution)/shard_map/all_to_all | solution.py:13
  423.5 91.3 %copy-start.10 = (s32[128,1]{0,1:T(1,128)S(1)}, s32[128,1]{0,1:T(1,128)}, u32[]{:S(2)}) copy-start(s32[128,1]{0,1:T(1,128)} %copy-done.9) | copy-start | bytes 1540
  508.9 19.8 %copy-start.8 = (s32[32,8]{1,0:T(8,128)S(1)}, s32[32,8]{1,0:T(8,128)}, u32[]{:S(2)}) copy-start(s32[32,8]{1,0:T(8,128)} %get-tuple-element.7) | copy-start | bytes 3076
  514.8 71.5 %copy-start.3 = (f32[8,2048]{1,0:T(8,128)S(1)}, f32[8,2048]{1,0:T(8,128)}, u32[]{:S(2)}) copy-start(f32[8,2048]{1,0:T(8,128)} %copy-done.2) | copy-start | bytes 196612
  514.8 71.5 %copy-start.5 = (f32[8,2048]{1,0:T(8,128)S(1)}, f32[8,2048]{1,0:T(8,128)}, u32[]{:S(2)}) copy-start(f32[8,2048]{1,0:T(8,128)} %copy-done.4) | copy-start | bytes 196612
  524.5 38.1 %all-to-all-start.4 = ((bf16[8,32,8,128]{3,2,0,1:T(8,128)(2,1)}), bf16[8,32,8,128]{3,2,0,1:T(8,128)(2,1)S(1)}, u32[]{:S(2)}, u32[]{:S(2)}) async-start(bf16[8,32,8,128]{3,2,0,1:T(8,128)(2,1)} %copy.97), calls=%async_computation.4 | async-start | bytes 1048576 | tf_op jit(solution)/shard_map/all_to_all | solution.py:162
where the time goes:
time: 599 us; the launch traced here: 598 us
  other arithmetic  278 us (46%)
  local copies, waits for them, and re-layouts  148 us (25%)
  waiting for transfers between devices  89.2 us (15%)
  starting transfers between devices  42.9 us (7%)
  blocking collectives  27.8 us (5%)
  matrix products  10.4 us (2%)
    scatter-add x1, other arithmetic, spread(): blank_grid = blank_grid.at[:, flat_low].add((1.0 - fractions) * weighted)  91.3 us
    scatter-add x1, other arithmetic, spread(): return blank_grid.at[:, flat_low + 1].add(fractions * weighted)  85.3 us
    gather x1, local copies, waits for them, and re-layouts, interpolate(): flat_values[:, flat_low + 1]  57.8 us
    gather x1, local copies, waits for them, and re-layouts, interpolate(): flat_values[:, flat_low]  57.8 us
    reduce_sum x1, other arithmetic, local(): partial_value = jnp.sum(own_turn * values, axis=0)  39 us
    all_to_all x1, waiting for transfers between devices, local(): lax.all_to_all(back_slots.reshape(local_orders, ma_count, capacity, block...  33.9 us
    mul x1, other arithmetic, spread(): return blank_grid.at[:, flat_low + 1].add(fractions * weighted)  33.4 us
    all_to_all x1, waiting for transfers between devices, local(): lax.all_to_all(outgoing.reshape(local_orders, ma_count, capacity, block_c...  30.8 us
  transfers between devices with their start and end apart: 5, of which 5 were waited for; matrix products, arithmetic and copies ran while one was open for 3% of the time, Pallas kernels for 0%

commit v1 on v0

--- a/solution.py
+++ b/solution.py
@@ -6,6 +6,13 @@
 
 PHI = 4096
 CELLS = 128
+
+
+def swap_blocks(block, axis, split, join):
+    n_dev = lax.axis_size(axis)
+    parts = jnp.stack(jnp.split(block, n_dev, axis=split), axis=0)
+    parts = lax.all_to_all(parts, axis, split_axis=0, concat_axis=0)
+    return jnp.concatenate(parts, axis=join)
 
 
 def copy_for_each(array, axis):
@@ -131,12 +138,11 @@
         axis=1,
     )
     outgoing = outgoing * (wanted_flat >= 0).astype(jnp.float32)[None, :, None]
-    incoming = lax.all_to_all(
+    incoming = swap_blocks(
         outgoing.reshape(local_orders, ma_count, capacity, block_cells).astype(jnp.bfloat16),
         "ma",
-        split_axis=1,
-        concat_axis=1,
-        tiled=True,
+        1,
+        1,
     ).astype(jnp.float32)
     blocks = jnp.take(
         incoming.reshape(local_orders, ma_count * capacity, block_cells), slot_index, axis=1

time: 599 us -> 616 us (1.028)
  local copies, waits for them, and re-layouts: 148 us -> 168 us
    unnamed x23 -> x54, local copies, waits for them, and re-layouts: 0.06 us -> 18.7 us
where the time goes in v1:
time: 616 us; the launch traced here: 614 us
  other arithmetic  276 us (45%)
  local copies, waits for them, and re-layouts  168 us (27%)
  waiting for transfers between devices  89.2 us (14%)
  starting transfers between devices  42 us (7%)
  blocking collectives  27.8 us (5%)
  matrix products  10.4 us (2%)
    scatter-add x1, other arithmetic, spread(): blank_grid = blank_grid.at[:, flat_low].add((1.0 - fractions) * weighted)  91.3 us
    scatter-add x1, other arithmetic, spread(): return blank_grid.at[:, flat_low + 1].add(fractions * weighted)  85.3 us
    gather x1, local copies, waits for them, and re-layouts, interpolate(): flat_values[:, flat_low + 1]  57.8 us
    gather x1, local copies, waits for them, and re-layouts, interpolate(): flat_values[:, flat_low]  57.8 us
    reduce_sum x1, other arithmetic, local(): partial_value = jnp.sum(own_turn * values, axis=0)  39 us
    all_to_all x1, waiting for transfers between devices, local(): lax.all_to_all(back_slots.reshape(local_orders, ma_count, capacity, block...  33.9 us
    mul x1, other arithmetic, spread(): return blank_grid.at[:, flat_low + 1].add(fractions * weighted)  33.4 us
    all_to_all x1, waiting for transfers between devices, swap_blocks(): parts = lax.all_to_all(parts, axis, split_axis=0, concat_axis=0)  30.8 us
  transfers between devices with their start and end apart: 5, of which 5 were waited for; matrix products, arithmetic and copies ran while one was open for 3% of the time, Pallas kernels for 0%

profile of v1, /device:TPU:2, one launch (start us, length us, event | category | flops | bytes accessed | tf_op | source)
XLA Modules:
  0.0 614.5 jit_solution(18272472430506424719)
XLA Ops:
  0.0 0.8 fusion.47
  0.9 0.8 select_reduce_fusion
  1.8 1.2 and_bitcast_fusion
  3.0 1.1 scatter_custom_fusion
  4.1 0.7 all_to_all.44
  4.8 15.5 %all-to-all-start = ((s32[32,1,8]{2,1,0:T(1,128)}), s32[32,1,8]{2,1,0:T(1,128)S(1)}, u32[]{:S(2)}, u32[]{:S(2)}) async-start(s32[32,1,8]{2,1,0:T(1,128)} %bitcast.12), calls=%async_computation | async-start | bytes 32768 | tf_op jit(solution)/shard_map/all_to_all | solution.py:133
  20.3 1.1 fusion.71
  21.4 0.9 fusion.72
  22.3 4.8 fusion.33
  27.5 3.4 fusion.36
  30.8 0.8 copy.192
  31.6 1.1 all-to-all-done
  32.7 11.1 %all-to-all-start.1 = ((f32[8,2,2,64]{0,2,1,3:T(2,128)}), f32[8,2,2,64]{0,2,1,3:T(2,128)S(1)}, u32[]{:S(2)}, u32[]{:S(2)}) async-start(f32[8,2,2,64]{0,2,1,3:T(2,128)} %copy.192), calls=%async_computation.1 | async-start | bytes 262144 | tf_op jit(solution)/shard_map/all_to_all | solution.py:114
  44.4 1.3 fusion.67
  47.0 14.0 %all-to-all-done.1 = f32[8,2,2,64]{0,2,1,3:T(2,128)S(1)} async-done(((f32[8,2,2,64]{0,2,1,3:T(2,128)}), f32[8,2,2,64]{0,2,1,3:T(2,128)S(1)}, u32[]{:S(2)}, u32[]{:S(2)}) %all-to-all-start.1) | async-done | bytes 8224 | tf_op jit(solution)/shard_map/all_to_all | solution.py:114
  61.1 1.2 fusion.12
  62.3 1.2 gather_fusion
  63.5 1.0 fusion.25
  71.1 0.6 constant_dynamic-update-slice_fusion.20
  72.9 0.6 constant_dynamic-update-slice_fusion.17
  77.7 0.6 constant_dynamic-update-slice_fusion.9
  83.7 4.1 all-to-all-start.2
  87.8 0.6 pad_clamp_fusion
  88.4 0.7 broadcast_bitcast_fusion
  89.2 1.6 broadcast_clamp_fusion
  90.8 30.8 %all-to-all-done.2 = bf16[32,8,1,8,128]{4,3,1,2,0:T(8,128)(2,1)S(1)} async-done(((bf16[32,8,1,8,128]{4,3,1,2,0:T(8,128)(2,1)}), bf16[32,8,1,8,128]{4,3,1,2,0:T(8,128)(2,1)S(1)}, u32[]{:S(2)}, u32[]{:S(2)}) %all-to-all-start.2) | async-done | bytes 524320 | tf_op jit(solution)/shard_map/all_to_all | solution.py:14
  121.6 0.6 copy.200
  122.2 1.5 gather_fusion.1
  123.8 5.7 copy.201
  129.4 13.1 %broadcast_select_fusion = f32[8,16384]{0,1:T(8,128)} fusion(f32[8,16384]{0,1:T(8,128)} %copy.201, pred[16384]{0:T(1024)(128)(4,1)S(1)} %broadcast_bitcast_fusion), kind=kLoop, calls=%fused_computation.17 | loop fusion | flops 131072 | bytes 1064960 | tf_op jit(solution)/shard_map/jit(_take)/select_n | solution.py:147
  142.6 57.8 %gather_fusion.2 = f32[16384,8]{1,0:T(8,128)} fusion(f32[8,16384]{0,1:T(8,128)} %broadcast_select_fusion, s32[16384]{0:T(1024)S(1)} %copy-done.7), kind=kCustom, calls=%fused_computation.2 | custom fusion | bytes 1114112 | tf_op jit(solution)/shard_map/gather | solution.py:78
  200.4 57.8 %gather_fusion.3 = f32[16384,8]{1,0:T(8,128)} fusion(f32[8,16384]{0,1:T(8,128)} %broadcast_select_fusion, s32[16384]{0:T(1024)S(1)} %get-tuple-element.11), kind=kCustom, calls=%fused_computation.3 | custom fusion | bytes 1114112 | tf_op jit(solution)/shard_map/gather | solution.py:78
  258.2 39.0 %fusion.6 = bf16[128,128]{1,0:T(8,128)(2,1)S(1)} fusion(f32[128,128,8]{2,1,0:T(8,128)} %bitcast.260, f32[128,128,8]{2,1,0:T(8,128)} %bitcast.259, f32[128,128]{1,0:T(8,128)S(1)} %bitcast.267, f32[128,128]{1,0:T(8,128)S(1)} %broadcast_subtract_fusion, f32[128,128]{1,0:T(8,128)S(1)} %bitcast.271, f32[8]{0:T(128)S(1)} %fusion.58, pred[8]{0:T(512)(128)(4,1)S(1)} %fusion.54), kind=kLoop, calls=%fused_computation.16 | loop fusion | flops 1032192 | bytes 1277992 | tf_op jit(solution)/shard_map/reduce_sum | solution.py:155
  297.1 0.9 broadcast_in_dim.73
  298.0 7.5 %all-to-all-start.3 = ((bf16[16,128,128]{2,1,0:T(8,128)(2,1)}), bf16[16,128,128]{2,1,0:T(8,128)(2,1)S(1)}, u32[]{:S(2)}, u32[]{:S(2)}) async-start(bf16[16,128,128]{2,1,0:T(8,128)(2,1)} %broadcast_in_dim.73), calls=%async_computation.3 | async-start | bytes 1048576 | tf_op jit(solution)/shard_map/all_to_all | solution.py:20
  306.1 9.4 %all-to-all-done.3 = bf16[16,128,128]{2,1,0:T(8,128)(2,1)S(1)} async-done(((bf16[16,128,128]{2,1,0:T(8,128)(2,1)}), bf16[16,128,128]{2,1,0:T(8,128)(2,1)S(1)}, u32[]{:S(2)}, u32[]{:S(2)}) %all-to-all-start.3) | async-done | bytes 524320 | tf_op jit(solution)/shard_map/all_to_all | solution.py:20
  315.9 33.4 %fusion.3 = (f32[8,128,128]{0,2,1:T(8,128)}, f32[8,128,128]{0,2,1:T(8,128)}) fusion(f32[128,128]{1,0:T(8,128)S(1)} %fusion.14, f32[128,128]{1,0:T(8,128)S(1)} %bitcast.268, f32[128,128]{1,0:T(8,128)S(1)} %bitcast.272, f32[8]{0:T(128)S(1)} %fusion.58, pred[8]{0:T(512)(128)(4,1)S(1)} %fusion.54, f32[128,128]{1,0:T(8,128)S(1)} %broadcast_subtract_fusion), kind=kLoop, calls=%fused_computation.13 | loop fusion | flops 655360 | bytes 1310760 | tf_op jit(solution)/shard_map/mul | solution.py:84
  349.3 91.3 %scatter_custom_fusion.1 = f32[8,16384]{0,1:T(8,128)} fusion(s32[16384]{0:T(1024)} %get-tuple-element.24, f32[16384,8]{1,0:T(8,128)} %bitcast.261, f32[]{:T(128)} %constant.97.clone.1), kind=kCustom, calls=%fused_computation.18 | custom fusion | flops 131072 | bytes 524800 | tf_op jit(solution)/shard_map/scatter-add | solution.py:83
  440.6 85.3 %scatter_fusion = f32[8,16384]{0,1:T(8,128)} fusion(f32[8,16384]{0,1:T(8,128)} %scatter_custom_fusion.1, s32[16384]{0:T(1024)S(1)} %get-tuple-element.12, f32[16384,8]{1,0:T(8,128)} %bitcast.258), kind=kCustom, calls=%fused_computation.6 | custom fusion | flops 131072 | bytes 1638400 | tf_op jit(solution)/shard_map/scatter-add | solution.py:84
  525.9 5.9 copy.202
  531.9 8.7 %scatter_fusion.1 = f32[8,256,128]{2,0,1:T(8,128)S(1)} fusion(f32[8,256,128]{2,0,1:T(8,128)S(1)} %broadcast_in_dim.40, s32[128]{0:T(128)S(1)} %bitcast.283, f32[128,8,128]{2,1,0:T(8,128)} %bitcast.264), kind=kCustom, calls=%fused_computation.7 | custom fusion | bytes 1573376 | tf_op jit(solution)/shard_map/scatter | solution.py:166
  540.7 0.9 copy.203
  541.6 3.9 all-to-all-start.4
  545.6 33.9 %all-to-all-done.4 = bf16[8,32,8,128]{3,2,0,1:T(8,128)(2,1)S(1)} async-done(((bf16[8,32,8,128]{3,2,0,1:T(8,128)(2,1)}), bf16[8,32,8,128]{3,2,0,1:T(8,128)(2,1)S(1)}, u32[]{:S(2)}, u32[]{:S(2)}) %all-to-all-start.4) | async-done | bytes 524320 | tf_op jit(solution)/shard_map/all_to_all | solution.py:168
  579.8 2.5 fusion.18
  582.5 17.3 %all_to_all.65 = bf16[8,64,2,2]{0,3,2,1:T(2,128)(2,1)S(1)} all-to-all(bf16[8,64,2,2]{0,3,2,1:T(2,128)(2,1)S(1)} %copy.206), channel_id=1, replica_groups=mesh['beam'=16,'ma'=32] {'ma'}, dimensions={1} | all-to-all | bytes 8192 | tf_op jit(solution)/shard_map/all_to_all | solution.py:188
  600.0 2.8 fusion.73
  603.3 10.5 %all_to_all.66 = bf16[16,2,2,128]{3,1,2,0:T(2,128)(2,1)S(1)} all-to-all(bf16[16,2,2,128]{3,1,2,0:T(2,128)(2,1)S(1)} %maximum_bitcast_fusion), channel_id=1, replica_groups=mesh['beam'=16,'ma'=32] {'beam'}, dimensions={0} | all-to-all | bytes 32768 | tf_op jit(solution)/shard_map/all_to_all | solution.py:37
  (84 shorter events, 22.3 us)
Async XLA Ops:
  0.0 315.6 %copy-start = (f32[128,128]{1,0:T(8,128)S(1)}, f32[128,128]{1,0:T(8,128)}, u32[]{:S(2)}) copy-start(f32[128,128]{1,0:T(8,128)} %param.21) | copy-start | bytes 196612
  3.0 18.4 %copy-start.9 = (s32[128,1]{0,1:T(1,128)}, s32[128,1]{0,1:T(1,128)S(1)}, u32[]{:S(2)}) copy-start(s32[128,1]{0,1:T(1,128)S(1)} %get-tuple-element.14) | copy-start | bytes 1540
  4.8 28.0 %all-to-all-start = ((s32[32,1,8]{2,1,0:T(1,128)}), s32[32,1,8]{2,1,0:T(1,128)S(1)}, u32[]{:S(2)}, u32[]{:S(2)}) async-start(s32[32,1,8]{2,1,0:T(1,128)} %bitcast.12), calls=%async_computation | async-start | bytes 32768 | tf_op jit(solution)/shard_map/all_to_all | solution.py:133
  21.4 67.0 %copy-start.1 = (f32[16384]{0:T(1024)S(1)}, f32[16384]{0:T(1024)}, u32[]{:S(2)}) copy-start(f32[16384]{0:T(1024)} %param.18) | copy-start | bytes 196612
  27.1 34.0 %copy-start.2 = (f32[8,2048]{1,0:T(8,128)}, f32[8,2048]{1,0:T(8,128)S(1)}, u32[]{:S(2)}) copy-start(f32[8,2048]{1,0:T(8,128)S(1)} %get-tuple-element.30) | copy-start | bytes 196612
  27.1 34.0 %copy-start.4 = (f32[8,2048]{1,0:T(8,128)}, f32[8,2048]{1,0:T(8,128)S(1)}, u32[]{:S(2)}) copy-start(f32[8,2048]{1,0:T(8,128)S(1)} %get-tuple-element.31) | copy-start | bytes 196612
  32.7 28.3 %all-to-all-start.1 = ((f32[8,2,2,64]{0,2,1,3:T(2,128)}), f32[8,2,2,64]{0,2,1,3:T(2,128)S(1)}, u32[]{:S(2)}, u32[]{:S(2)}) async-start(f32[8,2,2,64]{0,2,1,3:T(2,128)} %copy.192), calls=%async_computation.1 | async-start | bytes 262144 | tf_op jit(solution)/shard_map/all_to_all | solution.py:114
  83.7 37.9 %all-to-all-start.2 = ((bf16[32,8,1,8,128]{4,3,1,2,0:T(8,128)(2,1)}), bf16[32,8,1,8,128]{4,3,1,2,0:T(8,128)(2,1)S(1)}, u32[]{:S(2)}, u32[]{:S(2)}) async-start(bf16[32,8,1,8,128]{4,3,1,2,0:T(8,128)(2,1)} %constant_dynamic-update-slice_fusion), calls=%async_computation.2 | async-start | bytes 1048576 | tf_op jit(solution)/shard_map/all_to_all | solution.py:14
  129.4 13.1 %copy-start.7 = (s32[16384]{0:T(1024)S(1)}, s32[16384]{0:T(1024)}, u32[]{:S(2)}) copy-start(s32[16384]{0:T(1024)} %get-tuple-element.23) | copy-start | bytes 196612
  142.6 115.6 %copy-start.6 = (f32[16384]{0:T(1024)S(1)}, f32[16384]{0:T(1024)}, u32[]{:S(2)}) copy-start(f32[16384]{0:T(1024)} %param.19) | copy-start | bytes 196612
  298.0 17.5 %all-to-all-start.3 = ((bf16[16,128,128]{2,1,0:T(8,128)(2,1)}), bf16[16,128,128]{2,1,0:T(8,128)(2,1)S(1)}, u32[]{:S(2)}, u32[]{:S(2)}) async-start(bf16[16,128,128]{2,1,0:T(8,128)(2,1)} %broadcast_in_dim.73), calls=%async_computation.3 | async-start | bytes 1048576 | tf_op jit(solution)/shard_map/all_to_all | solution.py:20
  440.6 91.3 %copy-start.10 = (s32[128,1]{0,1:T(1,128)S(1)}, s32[128,1]{0,1:T(1,128)}, u32[]{:S(2)}) copy-start(s32[128,1]{0,1:T(1,128)} %copy-done.9) | copy-start | bytes 1540
  525.9 19.6 %copy-start.8 = (s32[32,8]{1,0:T(8,128)S(1)}, s32[32,8]{1,0:T(8,128)}, u32[]{:S(2)}) copy-start(s32[32,8]{1,0:T(8,128)} %get-tuple-element.7) | copy-start | bytes 3076
  531.8 71.3 %copy-start.3 = (f32[8,2048]{1,0:T(8,128)S(1)}, f32[8,2048]{1,0:T(8,128)}, u32[]{:S(2)}) copy-start(f32[8,2048]{1,0:T(8,128)} %copy-done.2) | copy-start | bytes 196612
  531.8 71.3 %copy-start.5 = (f32[8,2048]{1,0:T(8,128)S(1)}, f32[8,2048]{1,0:T(8,128)}, u32[]{:S(2)}) copy-start(f32[8,2048]{1,0:T(8,128)} %copy-done.4) | copy-start | bytes 196612
  541.6 37.9 %all-to-all-start.4 = ((bf16[8,32,8,128]{3,2,0,1:T(8,128)(2,1)}), bf16[8,32,8,128]{3,2,0,1:T(8,128)(2,1)S(1)}, u32[]{:S(2)}, u32[]{:S(2)}) async-start(bf16[8,32,8,128]{3,2,0,1:T(8,128)(2,1)} %copy.203), calls=%async_computation.4 | async-start | bytes 1048576 | tf_op jit(solution)/shard_map/all_to_all | solution.py:168
